TPU v7x, 32 devices: a whole 2x2x4 slice. The times are simulated.
32 devices in a mesh: seq: 8 (over z, x), head: 4 (over y, core).
Axes of the slice: x: 2, y: 2, z: 4, core: 2. Of those that a mesh axis runs over, the one named last changes fastest.
Arguments:
- x_in: bfloat16 [2048, 4096], P('seq', 'head'), may hold values from -6 to 6
- z_gate: bfloat16 [2048, 4096], P('seq', 'head'), may hold values from -8 to 8
- b_proj: bfloat16 [2048, 4, 256], P('seq', 'head'), may hold values from -6 to 6
- c_proj: bfloat16 [2048, 4, 256], P('seq', 'head'), may hold values from -6 to 6
- log_decay: float32 [2048, 64], P('seq', 'head'), may hold values from -1 to 0
- norm_gain: float32 [4096], P('head'), may hold values from 0.5 to 1.5
- w_out: bfloat16 [4096, 8192], P('head', 'seq'), may hold values from -0.125 to 0.125
Outputs:
- mixed: bfloat16 [2048, 8192], P('seq', 'head')
All inputs are finite; a program needn't handle non-finite values.
Results may differ from a plain program's by a relative error of at most 0.015.
Values may be sent and summed in bfloat16 or wider, within the bound.
No kernel may reach another device: no remote copies, remote signals or barrier semaphores. Data moves between devices by JAX's collectives and lax.ppermute only.
A program may use at most 128 MiB of HBM per device.

v0:
```python
import jax
import jax.numpy as jnp
from jax import lax
from jax.sharding import PartitionSpec as P


def carried_in(value, axis, combine, identity):
    count, place = (lax.axis_size(axis), lax.axis_index(axis))
    everything = jax.tree.map(
        lambda part, kind: lax.all_gather(part.astype(kind), axis),
        value,
        (jnp.bfloat16, jnp.bfloat16),
    )
    start = jax.tree.map(
        lambda part, zero: jnp.broadcast_to(jnp.asarray(zero, part.dtype), part.shape),
        value,
        identity,
    )

    def hop(k, before):
        reached = k < place
        new = combine(
            before, jax.tree.map(lambda part, own: part[k].astype(own.dtype), everything, value)
        )
        return jax.tree.map(lambda a, b: jnp.where(reached, a, b), new, before)

    return lax.fori_loop(0, count, hop, start)


def combine(earlier, later):
    return (earlier[0] * later[0], later[0][:, None, None] * earlier[1] + later[1])


def carry_in(decay_total, state):
    identity = (jnp.ones_like(decay_total), jnp.zeros_like(state))
    return carried_in((decay_total, state), "seq", combine, identity)


def body(x_in, z_gate, b_proj, c_proj, log_decay, norm_gain, w_out):
    rows = x_in.shape[0]
    heads = log_decay.shape[1]
    head_dim = x_in.shape[1] // heads
    b_local = b_proj[:, 0, :]
    c_local = c_proj[:, 0, :]
    x_heads = x_in.reshape(rows, heads, head_dim)
    cum = jnp.cumsum(log_decay, axis=0)
    total = cum[-1]
    scores = jnp.dot(c_local, b_local.T, preferred_element_type=jnp.float32)
    index = jnp.arange(rows)
    causal = (index[:, None] >= index[None, :])[None]
    cum_t = cum.T
    diff = cum_t[:, :, None] - cum_t[:, None, :]
    mask = jnp.where(causal, jnp.exp(jnp.where(causal, diff, 0.0)), 0.0)
    weighted = (mask * scores[None]).astype(jnp.bfloat16)
    y_intra = jnp.einsum("hij,jhp->ihp", weighted, x_heads, preferred_element_type=jnp.float32)
    weights = jnp.exp(total[None, :] - cum)
    scaled = (weights[:, :, None] * x_heads.astype(jnp.float32)).astype(jnp.bfloat16)
    state = jnp.einsum("thp,tn->hpn", scaled, b_local, preferred_element_type=jnp.float32)
    carried = carry_in(jnp.exp(total), state)
    state_in = carried[1].astype(jnp.bfloat16)
    y_state = jnp.exp(cum)[:, :, None] * jnp.einsum(
        "tn,hpn->thp", c_local, state_in, preferred_element_type=jnp.float32
    )
    y_all = (y_intra + y_state).reshape(rows, heads * head_dim)
    gated = y_all * jax.nn.silu(z_gate.astype(jnp.float32))
    mean_sq = jnp.mean(gated * gated, axis=1, keepdims=True)
    hidden = (gated * lax.rsqrt(mean_sq + 1e-05) * norm_gain[None, :]).astype(jnp.bfloat16)
    partial_terms = jnp.dot(
        hidden, lax.all_gather(w_out, "seq", axis=1, tiled=True), preferred_element_type=jnp.float32
    )
    mixed = lax.psum_scatter(
        partial_terms.astype(jnp.bfloat16), "head", scatter_dimension=1, tiled=True
    )
    return mixed


def solution(mesh):
    placed = (
        P("seq", "head"),
        P("seq", "head"),
        P("seq", "head", None),
        P("seq", "head", None),
        P("seq", "head"),
        P("head"),
        P("head", "seq"),
    )
    return jax.shard_map(
        body, mesh=mesh, in_specs=placed, out_specs=P("seq", "head"), check_vma=False
    )
```

profile of v0, /device:TPU:0, one launch (start us, length us, event | category | flops | bytes accessed | tf_op | source)
XLA Modules:
  0.0 377.3 jit_solution(7258897654931674551)
XLA Ops:
  6.5 0.0 copy-start
  6.5 0.0 copy-start.1
  6.5 0.0 all-gather.7.cloned.1.call-start
  6.5 0.8 copy_bitcast_fusion.1
  7.3 0.6 reduce-window.6
  7.9 0.2 slice_reduce_fusion
  8.1 0.1 fusion.25
  8.2 0.2 slice_reduce_fusion.1
  8.3 0.1 bitcast_exponential_fusion
  8.4 1.2 copy.27
  9.7 0.1 fusion.14
  9.8 0.0 copy-done
  9.8 1.1 convolution_convert_fusion.1
  10.9 0.0 all-gather.7.cloned.1.call-update
  10.9 0.0 all-gather.5.cloned.1.call-start
  11.0 0.7 all-gather.5.cloned.1.call-update
  11.7 0.0 reduce-scatter.2.cloned.1.call-start
  11.7 0.2 fusion.23
  11.9 22.2 %all-gather.1 = bf16[8,1,16]{2,1,0:T(2,128)(2,1)S(1)} all-gather(bf16[1,1,16]{2,1,0:T(2,128)(2,1)S(1)} %bitcast.72), channel_id=1, replica_groups=mesh['seq'=8,'head'=4] {'seq'}, dimensions={0}, use_global_device_ids=true | all-gather | bytes 288 | tf_op jit(solution)/shard_map/all_gather | solution.py:10
  34.2 0.0 copy-done.1
  34.2 0.2 fusion.20
  34.4 1.2 fusion.7
  35.6 51.5 %all-gather.7.cloned.1.call-done = bf16[128,64,256]{2,1,0:T(8,128)(2,1)} async-done(((bf16[16,64,256]{2,1,0:T(8,128)(2,1)}), bf16[128,64,256]{2,1,0:T(8,128)(2,1)}) %all-gather.7.cloned.1.call-update) | async-done | bytes 4194320 | tf_op jit(solution)/shard_map/all_gather | solution.py:10
  87.2 10.9 %while.14 = (s32[]{:T(128)}, f32[16,64,256]{2,1,0:T(8,128)S(1)}, s32[]{:T(128)}, bf16[8,16]{1,0:T(8,128)(2,1)S(1)}, bf16[8,16,64,256]{3,2,1,0:T(8,128)(2,1)}, /*index=5*/s32[]{:T(128)}, s32[]{:T(128)}) while((s32[]{:T(128)}, f32[16,64,256]{2,1,0:T(8,128)S(1)}, s32[]{:T(128)}, bf16[8,16]{1,0:T(8,128)(2,1)S(1)}, ...), condition=%wide.region_3.4_spmd.clone, body=%wide.region_2.3_spmd.clone.sunk | while | flops 1310740 | bytes 2621705 | solution.py:27
  87.2 1.3 fusion.32
  88.5 1.3 fusion.32
  89.8 1.3 fusion.32
  91.2 1.3 fusion.32
  92.5 1.3 fusion.32
  93.8 1.4 fusion.32
  95.3 1.4 fusion.32
  96.7 1.3 fusion.32
  98.0 0.0 copy-start.2
  98.1 0.4 fusion.9
  98.4 0.3 copy.29
  98.8 1.6 multiply_reduce_fusion
  100.3 214.9 %all-gather.5.cloned.1.call-done = bf16[1024,8192]{1,0:T(8,128)(2,1)} async-done(((bf16[1024,1024]{1,0:T(8,128)(2,1)}), bf16[1024,8192]{1,0:T(8,128)(2,1)}) %all-gather.5.cloned.1.call-update) | async-done | bytes 16777232 | tf_op jit(solution)/shard_map/all_gather | solution.py:69
  315.3 0.0 copy-done.2
  315.3 12.6 %convolution_convert_fusion = bf16[256,8192]{1,0:T(8,128)(2,1)} fusion(bf16[1024,8192]{1,0:T(8,128)(2,1)} %all-gather.5.cloned.1.call-done, f32[1024]{0:T(1024)S(1)} %copy-done.2, f32[256]{0:T(256)S(1)} %add_rsqrt_fusion, f32[256,1024]{1,0:T(8,128)S(1)} %copy.29, bf16[256,1024]{1,0:T(8,128)(2,1)} %param.10), kind=kOutput, calls=%fused_computation.3 | convolution fusion | flops 4299423744 | bytes 22549504 | tf_op jit(solution)/shard_map/dot_general | solution.py:68
  327.9 0.0 reduce-scatter.2.cloned.1.call-update
  327.9 42.8 %reduce-scatter.2.cloned.1.call-done = bf16[256,2048]{1,0:T(8,128)(2,1)} async-done(((bf16[256,8192]{1,0:T(8,128)(2,1)}), bf16[256,2048]{1,0:T(8,128)(2,1)}) %reduce-scatter.2.cloned.1.call-update) | async-done | bytes 1048592 | tf_op jit(solution)/shard_map/reduce_scatter | solution.py:71
  (14 shorter events, 0.1 us)
Async XLA Ops:
  6.5 3.3 copy-start
  6.5 27.7 %copy-start.1 = (bf16[256,1,256]{2,0,1:T(8,128)(2,1)S(1)}, bf16[256,1,256]{2,0,1:T(8,128)(2,1)}, u32[]{:S(2)}) copy-start(bf16[256,1,256]{2,0,1:T(8,128)(2,1)} %param.12) | copy-start | bytes 393220
  6.5 80.6 %all-gather.7.cloned.1.call-start = ((), (), s32[]{:S(2)}) async-start(), calls=%async_computation.3 | async-start | bytes 4718592 | tf_op jit(solution)/shard_map/all_gather | solution.py:10
  10.9 304.3 %all-gather.5.cloned.1.call-start = ((), (), s32[]{:S(2)}) async-start(), calls=%async_computation.1 | async-start | bytes 18874368 | tf_op jit(solution)/shard_map/all_gather | solution.py:69
  11.7 359.1 %reduce-scatter.2.cloned.1.call-start = ((), (), s32[]{:S(2)}) async-start(), calls=%async_computation.2 | async-start | bytes 5242880 | tf_op jit(solution)/shard_map/reduce_scatter | solution.py:71
  98.0 217.2 %copy-start.2 = (f32[1024]{0:T(1024)S(1)}, f32[1024]{0:T(1024)}, u32[]{:S(2)}) copy-start(f32[1024]{0:T(1024)} %param.14) | copy-start | bytes 12292
Sparse Core Ops, SparseCore 0:
  11.0 76.0 all-gather.6
  89.4 225.8 all-gather.4
  328.0 42.6 reduce-scatter.1
where the time goes:
time: 378 us; the launch traced here: 377 us
  waiting for transfers between devices  310 us (82%)
  blocking collectives  22.2 us (6%)
  matrix products  15.5 us (4%)
  other arithmetic  13.3 us (4%)
  between operations  13.2 us (3%)
    all_gather x1, waiting for transfers between devices, body(): lax.all_gather(w_out, 'seq', axis=1, tiled=True)  215 us
    all_gather x1, waiting for transfers between devices, carried_in(): lax.all_gather(part.astype(kind), axis)  51.5 us
    reduce_scatter x1, waiting for transfers between devices, body(): lax.psum_scatter(partial_terms.astype(jnp.bfloat16), 'head', scatter_dime...  42.8 us
    all_gather x1, blocking collectives, carried_in(): lax.all_gather(part.astype(kind), axis)  22.2 us
    dot_general x1, matrix products, body(): jnp.dot(hidden, lax.all_gather(w_out, 'seq', axis=1, tiled=True), preferr...  12.6 us
    select_n x8, other arithmetic, hop(): return jax.tree.map(lambda a, b: jnp.where(reached, a, b), new, before)  10.6 us
  transfers between devices with their start and end apart: 3, of which 3 were waited for; matrix products, arithmetic and copies ran while one was open for 4% of the time, Pallas kernels for 0%

commit v1 on v0

--- a/solution.py
+++ b/solution.py
@@ -2,6 +2,19 @@
 import jax.numpy as jnp
 from jax import lax
 from jax.sharding import PartitionSpec as P
+
+
+def ring_gather(shard, axis, dim):
+    ways = lax.axis_size(axis)
+    up = [(d, (d + 1) % ways) for d in range(ways)]
+    down = [(d, (d - 1) % ways) for d in range(ways)]
+    earlier, later = ([shard], [shard])
+    for _ in range(ways // 2):
+        earlier.append(lax.ppermute(earlier[-1], axis, up))
+    for _ in range((ways - 1) // 2):
+        later.append(lax.ppermute(later[-1], axis, down))
+    line = jnp.concatenate([*earlier[::-1], *later[1:]], axis=dim)
+    return jnp.roll(line, (lax.axis_index(axis) - ways // 2) * shard.shape[dim], axis=dim)
 
 
 def carried_in(value, axis, combine, identity):
@@ -66,7 +79,7 @@
     mean_sq = jnp.mean(gated * gated, axis=1, keepdims=True)
     hidden = (gated * lax.rsqrt(mean_sq + 1e-05) * norm_gain[None, :]).astype(jnp.bfloat16)
     partial_terms = jnp.dot(
-        hidden, lax.all_gather(w_out, "seq", axis=1, tiled=True), preferred_element_type=jnp.float32
+        hidden, ring_gather(w_out, "seq", 1), preferred_element_type=jnp.float32
     )
     mixed = lax.psum_scatter(
         partial_terms.astype(jnp.bfloat16), "head", scatter_dimension=1, tiled=True

time: 378 us -> 483 us (1.28)
  local copies, waits for them, and re-layouts: 2.7 us -> 49.5 us
  blocking collectives: 22.2 us -> 58.3 us
  starting transfers between devices: 0.08 us -> 16.2 us
  matrix products: 15.5 us -> 20.5 us
    ppermute x0 -> x7, waiting for transfers between devices: none -> 266 us  [the longest x4 266 us: ring_gather(): earlier.append(lax.ppermute(earlier[-1], axis, up))]
    all_gather x1 -> x0, waiting for transfers between devices: 215 us -> none  [body(): lax.all_gather(w_out, 'seq', axis=1, tiled=True)]
    all_gather x1, waiting for transfers between devices: 51.5 us -> 0.01 us  [carried_in(): lax.all_gather(part.astype(kind), axis)]
    unnamed x8 -> x33, local copies, waits for them, and re-layouts: 1.26 us -> 43.8 us
    all_gather x1, blocking collectives: 22.2 us -> 58.3 us  [carried_in(): lax.all_gather(part.astype(kind), axis)]
    ppermute x0 -> x7, starting transfers between devices: none -> 16.2 us  [the longest x4 9.57 us: ring_gather(): earlier.append(lax.ppermute(earlier[-1], axis, up))]
  transfers between devices with their start and end apart: 3 -> 9, of which waited for: 3 -> 4; matrix products, arithmetic and copies ran while one was open for 4% -> 8% of each run, Pallas kernels for 0% -> 0%
where the time goes in v1:
time: 483 us; the launch traced here: 482 us
  waiting for transfers between devices  311 us (64%)
  blocking collectives  58.3 us (12%)
  local copies, waits for them, and re-layouts  49.5 us (10%)
  matrix products  20.5 us (4%)
  starting transfers between devices  16.2 us (3%)
  between operations  13.5 us (3%)
  other arithmetic  13.1 us (3%)
    ppermute x4, waiting for transfers between devices, ring_gather(): earlier.append(lax.ppermute(earlier[-1], axis, up))  266 us
    all_gather x1, blocking collectives, carried_in(): lax.all_gather(part.astype(kind), axis)  58.3 us
    reduce_scatter x1, waiting for transfers between devices, body(): lax.psum_scatter(partial_terms.astype(jnp.bfloat16), 'head', scatter_dime...  44.5 us
    unnamed x33, local copies, waits for them, and re-layouts  43.8 us
    dot_general x1, matrix products, body(): jnp.dot(hidden, ring_gather(w_out, 'seq', 1), preferred_element_type=jnp....  12.2 us
    select_n x8, other arithmetic, hop(): return jax.tree.map(lambda a, b: jnp.where(reached, a, b), new, before)  10.4 us
  transfers between devices with their start and end apart: 9, of which 4 were waited for; matrix products, arithmetic and copies ran while one was open for 8% of the time, Pallas kernels for 0%

profile of v1, /device:TPU:0, one launch (start us, length us, event | category | flops | bytes accessed | tf_op | source)
XLA Modules:
  0.0 482.2 jit_solution(8558035107834390081)
XLA Ops:
  6.5 1.4 copy.27
  7.9 0.7 copy_bitcast_fusion.1
  8.7 0.6 reduce-window.6
  9.9 1.1 convolution_convert_fusion
  11.1 3.0 collective-permute-start
  14.1 3.1 collective-permute-start.4
  17.2 113.2 %collective-permute-done = bf16[1024,1024]{1,0:T(8,128)(2,1)S(1)} collective-permute-done((bf16[1024,1024]{1,0:T(8,128)(2,1)}, bf16[1024,1024]{1,0:T(8,128)(2,1)S(1)}, u32[]{:S(2)}, u32[]{:S(2)}) %collective-permute-start) | collective-permute-done | bytes 2097184 | tf_op jit(solution)/shard_map/ppermute | solution.py:13
  130.4 1.3 copy-done.3
  131.7 2.4 collective-permute-start.1
  134.1 3.1 collective-permute-start.5
  137.2 85.0 %collective-permute-done.1 = bf16[1024,1024]{1,0:T(8,128)(2,1)} collective-permute-done((bf16[1024,1024]{1,0:T(8,128)(2,1)S(1)}, bf16[1024,1024]{1,0:T(8,128)(2,1)}, u32[]{:S(2)}, u32[]{:S(2)}) %collective-permute-start.1) | collective-permute-done | bytes 2097184 | tf_op jit(solution)/shard_map/ppermute | solution.py:13
  222.1 2.6 collective-permute-start.2
  224.9 58.3 %all-gather.1 = bf16[8,1,16]{2,1,0:T(2,128)(2,1)S(1)} all-gather(bf16[1,1,16]{2,1,0:T(2,128)(2,1)S(1)} %bitcast.71), channel_id=1, replica_groups=mesh['seq'=8,'head'=4] {'seq'}, dimensions={0}, use_global_device_ids=true | all-gather | bytes 288 | tf_op jit(solution)/shard_map/all_gather | solution.py:23
  283.2 1.1 fusion.25
  284.3 3.4 fusion.12
  287.7 0.4 collective-permute-start.6
  288.1 1.6 collective-permute-start.3
  289.8 10.7 %while.14 = (s32[]{:T(128)}, f32[16,64,256]{2,1,0:T(8,128)S(1)}, s32[]{:T(128)}, bf16[8,16]{1,0:T(8,128)(2,1)S(1)}, bf16[8,16,64,256]{3,2,1,0:T(8,128)(2,1)}, /*index=5*/s32[]{:T(128)}, s32[]{:T(128)}) while((s32[]{:T(128)}, f32[16,64,256]{2,1,0:T(8,128)S(1)}, s32[]{:T(128)}, bf16[8,16]{1,0:T(8,128)(2,1)S(1)}, ...), condition=%wide.region_3.4_spmd.clone, body=%wide.region_2.3_spmd.clone.sunk | while | flops 1310740 | bytes 2621713 | solution.py:40
  289.8 1.3 fusion.37
  291.1 1.3 fusion.37
  292.4 1.3 fusion.37
  293.8 1.3 fusion.37
  295.1 1.3 fusion.37
  296.4 1.3 fusion.37
  297.8 1.3 fusion.37
  299.1 1.3 fusion.37
  300.4 2.6 fusion.14
  303.0 1.6 copy.29
  304.6 1.6 multiply_reduce_fusion
  306.2 68.2 %collective-permute-done.3 = bf16[1024,1024]{1,0:T(8,128)(2,1)} collective-permute-done((bf16[1024,1024]{1,0:T(8,128)(2,1)}, bf16[1024,1024]{1,0:T(8,128)(2,1)}, u32[]{:S(2)}, u32[]{:S(2)}) %collective-permute-start.3) | collective-permute-done | bytes 2097184 | tf_op jit(solution)/shard_map/ppermute | solution.py:13
  374.4 3.0 constant_dynamic-update-slice_fusion.15
  377.5 3.0 constant_dynamic-update-slice_fusion.14
  380.5 3.1 constant_dynamic-update-slice_fusion.13
  383.6 3.1 constant_dynamic-update-slice_fusion.12
  386.7 1.5 constant_dynamic-update-slice_fusion.11
  388.1 3.0 constant_dynamic-update-slice_fusion.10
  391.2 3.1 constant_dynamic-update-slice_fusion.9
  394.3 3.0 constant_dynamic-update-slice_fusion.8
  397.3 3.1 constant_dynamic-update-slice_fusion.7
  400.4 3.1 constant_dynamic-update-slice_fusion.6
  403.4 3.1 constant_dynamic-update-slice_fusion.5
  406.5 1.5 constant_dynamic-update-slice_fusion.4
  408.0 1.5 constant_dynamic-update-slice_fusion.3
  409.4 3.1 constant_dynamic-update-slice_fusion.2
  412.5 3.0 constant_dynamic-update-slice_fusion.1
  415.6 3.1 constant_dynamic-update-slice_fusion
  418.6 12.2 %fusion.3 = bf16[256,8192]{1,0:T(8,128)(2,1)} fusion(bf16[1024,16384]{1,0:T(8,128)(2,1)} %constant_dynamic-update-slice_fusion, s32[]{:T(128)S(6)} %select_n.45, f32[1024]{0:T(1024)S(1)} %copy-done.7, f32[256]{0:T(256)S(1)} %add_rsqrt_fusion, f32[256,1024]{1,0:T(8,128)S(1)} %copy.29, bf16[256,1024]{1,0:T(8,128)(2,1)S(1)} %copy-done.6), kind=kOutput, calls=%fused_computation.5 | convolution fusion | flops 4299423744 | bytes 22549508 | tf_op jit(solution)/shard_map/dot_general | solution.py:81
  430.9 44.5 %reduce-scatter.2.cloned.1.call-done = bf16[256,2048]{1,0:T(8,128)(2,1)} async-done(((bf16[256,8192]{1,0:T(8,128)(2,1)}), bf16[256,2048]{1,0:T(8,128)(2,1)}) %reduce-scatter.2.cloned.1.call-update) | async-done | bytes 1048592 | tf_op jit(solution)/shard_map/reduce_scatter | solution.py:84
  (44 shorter events, 1.0 us)
Async XLA Ops:
  6.5 3.4 copy-start
  6.5 380.1 %copy-start.2 = (bf16[1024,1024]{1,0:T(8,128)(2,1)S(1)}, bf16[1024,1024]{1,0:T(8,128)(2,1)}, u32[]{:S(2)}) copy-start(bf16[1024,1024]{1,0:T(8,128)(2,1)} %param.15) | copy-start | bytes 6291460
  6.5 283.2 %all-gather.4.cloned.1.call-start = ((), (), s32[]{:S(2)}) async-start(), calls=%async_computation.2 | async-start | bytes 4718592 | tf_op jit(solution)/shard_map/all_gather | solution.py:23
  7.9 216.8 %copy-start.5 = (bf16[256,1024]{0,1:T(8,128)(2,1)}, bf16[256,1024]{0,1:T(8,128)(2,1)S(1)}, u32[]{:S(2)}) copy-start(bf16[256,1024]{0,1:T(8,128)(2,1)S(1)} %copy.27) | copy-start | bytes 1572868
  11.1 464.3 %reduce-scatter.2.cloned.1.call-start = ((), (), s32[]{:S(2)}) async-start(), calls=%async_computation.1 | async-start | bytes 5242880 | tf_op jit(solution)/shard_map/reduce_scatter | solution.py:84
  11.1 119.3 %collective-permute-start = (bf16[1024,1024]{1,0:T(8,128)(2,1)}, bf16[1024,1024]{1,0:T(8,128)(2,1)S(1)}, u32[]{:S(2)}, u32[]{:S(2)}) collective-permute-start(bf16[1024,1024]{1,0:T(8,128)(2,1)} %param.15), channel_id=1, source_target_pairs={{0,4},{4,8},{8,12},{12,16},{16,20},{20,24},{24,28},{28,0},{1,5},{5... | collective-permute-start | bytes 6291464 | tf_op jit(solution)/shard_map/ppermute | solution.py:13
  14.1 120.0 %collective-permute-start.4 = (bf16[1024,1024]{1,0:T(8,128)(2,1)}, bf16[1024,1024]{1,0:T(8,128)(2,1)}, u32[]{:S(2)}, u32[]{:S(2)}) collective-permute-start(bf16[1024,1024]{1,0:T(8,128)(2,1)} %param.15), channel_id=1, source_target_pairs={{0,28},{4,0},{8,4},{12,8},{16,12},{20,16},{24,20},{28,24},{1,29},{... | collective-permute-start | bytes 6291464 | tf_op jit(solution)/shard_map/ppermute | solution.py:15
  130.4 1.3 copy-start.3
  131.7 90.4 %collective-permute-start.1 = (bf16[1024,1024]{1,0:T(8,128)(2,1)S(1)}, bf16[1024,1024]{1,0:T(8,128)(2,1)}, u32[]{:S(2)}, u32[]{:S(2)}) collective-permute-start(bf16[1024,1024]{1,0:T(8,128)(2,1)S(1)} %collective-permute-done), channel_id=1, source_target_pairs={{0,4},{4,8},{8,12},{12,16},{16,20},{20,24},{24,28},{28,0},{1,5},{5... | collective-permute-start | bytes 6291464 | tf_op jit(solution)/shard_map/ppermute | solution.py:13
  134.1 153.6 %collective-permute-start.5 = (bf16[1024,1024]{1,0:T(8,128)(2,1)}, bf16[1024,1024]{1,0:T(8,128)(2,1)}, u32[]{:S(2)}, u32[]{:S(2)}) collective-permute-start(bf16[1024,1024]{1,0:T(8,128)(2,1)} %collective-permute-done.4), channel_id=1, source_target_pairs={{0,28},{4,0},{8,4},{12,8},{16,12},{20,16},{24,20},{28,24},{1,29},{... | collective-permute-start | bytes 6291464 | tf_op jit(solution)/shard_map/ppermute | solution.py:15
  222.1 66.0 %collective-permute-start.2 = (bf16[1024,1024]{1,0:T(8,128)(2,1)}, bf16[1024,1024]{1,0:T(8,128)(2,1)}, u32[]{:S(2)}, u32[]{:S(2)}) collective-permute-start(bf16[1024,1024]{1,0:T(8,128)(2,1)} %collective-permute-done.1), channel_id=1, source_target_pairs={{0,4},{4,8},{8,12},{12,16},{16,20},{20,24},{24,28},{28,0},{1,5},{5... | collective-permute-start | bytes 6291464 | tf_op jit(solution)/shard_map/ppermute | solution.py:13
  287.7 106.5 %collective-permute-start.6 = (bf16[1024,1024]{1,0:T(8,128)(2,1)}, bf16[1024,1024]{1,0:T(8,128)(2,1)}, u32[]{:S(2)}, u32[]{:S(2)}) collective-permute-start(bf16[1024,1024]{1,0:T(8,128)(2,1)} %collective-permute-done.5), channel_id=1, source_target_pairs={{0,28},{4,0},{8,4},{12,8},{16,12},{20,16},{24,20},{28,24},{1,29},{... | collective-permute-start | bytes 6291464 | tf_op jit(solution)/shard_map/ppermute | solution.py:15
  288.1 86.3 %collective-permute-start.3 = (bf16[1024,1024]{1,0:T(8,128)(2,1)}, bf16[1024,1024]{1,0:T(8,128)(2,1)}, u32[]{:S(2)}, u32[]{:S(2)}) collective-permute-start(bf16[1024,1024]{1,0:T(8,128)(2,1)} %collective-permute-done.2), channel_id=1, source_target_pairs={{0,4},{4,8},{8,12},{12,16},{16,20},{20,24},{24,28},{28,0},{1,5},{5... | collective-permute-start | bytes 6291464 | tf_op jit(solution)/shard_map/ppermute | solution.py:13
  304.6 101.9 %copy-start.4 = (bf16[1024,1024]{1,0:T(8,128)(2,1)S(1)}, bf16[1024,1024]{1,0:T(8,128)(2,1)}, u32[]{:S(2)}) copy-start(bf16[1024,1024]{1,0:T(8,128)(2,1)} %copy-done.3) | copy-start | bytes 6291460
  306.2 112.4 %copy-start.6 = (bf16[256,1024]{1,0:T(8,128)(2,1)S(1)}, bf16[256,1024]{1,0:T(8,128)(2,1)}, u32[]{:S(2)}) copy-start(bf16[256,1024]{1,0:T(8,128)(2,1)} %param.10) | copy-start | bytes 1572868
  306.2 112.4 %copy-start.7 = (f32[1024]{0:T(1024)S(1)}, f32[1024]{0:T(1024)}, u32[]{:S(2)}) copy-start(f32[1024]{0:T(1024)} %param.14) | copy-start | bytes 12292
  406.5 68.8 %copy-start.1 = (bf16[256,1,256]{2,0,1:T(8,128)(2,1)S(1)}, bf16[256,1,256]{2,0,1:T(8,128)(2,1)}, u32[]{:S(2)}) copy-start(bf16[256,1,256]{2,0,1:T(8,128)(2,1)} %param.11) | copy-start | bytes 393220
Sparse Core Ops, SparseCore 0:
  11.2 185.8 all-gather.3
  431.0 44.2 reduce-scatter.1
